TPU v7x, 256 devices: a whole 4x4x8 slice. The times are simulated.
256 devices in a mesh: cube: 4 (over y), grid: 64 (over z, x, core).
Axes of the slice: x: 4, y: 4, z: 8, core: 2. Of those that a mesh axis runs over, the one named last changes fastest.
Arguments:
- root_inverse: float32 [4096, 4096], P('grid', 'cube'), may hold values from -0.09375 to 0.09375
- level_inverse: float32 [1024, 2048], P('grid', 'cube'), may hold values from -0.1875 to 0.1875
- coupling: float32 [4096, 2048], P('grid', 'cube'), may hold values from -0.1875 to 0.1875
- pattern: int32 [2, 32], replicated, may hold values 0 or 1
Outputs:
- root_cov: float32 [4096, 4096], P('grid', 'cube')
- cross_cov: float32 [4096, 2048], P('grid', 'cube')
- node_cov: float32 [1024, 2048], P('grid', 'cube')
All inputs are finite; a program needn't handle non-finite values.
Results may differ from a plain program's by a relative error of at most 0.0001.
Values sent between devices are 32-bit elements; how exact they have to be, the bound alone decides.
No kernel may reach another device: no remote copies, remote signals or barrier semaphores. Data moves between devices by JAX's collectives and lax.ppermute only.
A program may use at most 128 MiB of HBM per device.

v0:
```python
import jax
import jax.numpy as jnp
from jax import lax
from jax.sharding import PartitionSpec as P

BLK = 128
HIGHEST = lax.Precision.HIGHEST


def from_partner(value, axis, apart):
    return lax.ppermute(value, axis, [(i, i ^ 1 << apart) for i in range(lax.axis_size(axis))])


def product(left, right):
    return jnp.dot(left, right, precision=HIGHEST, preferred_element_type=jnp.float32)


def lower_piece(weights, row_start, col_start):
    rows = row_start + lax.broadcasted_iota(jnp.int32, weights.shape, 0)
    cols = col_start + lax.broadcasted_iota(jnp.int32, weights.shape, 1)
    below = jnp.where(cols < rows, weights, jnp.zeros_like(weights))
    return below + jnp.where(cols == rows, 1.0, 0.0).astype(jnp.float32)


def join_halves(own, other, half):
    first = jnp.concatenate([own, other], axis=1)
    second = jnp.concatenate([other, own], axis=1)
    return jnp.where(half == 0, first, second)


def on_device(root_inverse, level_inverse, coupling, pattern):
    grid_index = lax.axis_index("grid")
    cube_index = lax.axis_index("cube")
    node = cube_index // 2
    half = cube_index % 2
    root_rows_dev, root_cols_dev = root_inverse.shape
    node_rows_dev, half_width = level_inverse.shape
    root_lower = lower_piece(root_inverse, grid_index * root_rows_dev, cube_index * root_cols_dev)
    node_lower = lower_piece(level_inverse, grid_index * node_rows_dev, half * half_width)
    row_ids = grid_index * root_rows_dev + jnp.arange(root_rows_dev, dtype=jnp.int32)
    block_count = pattern.shape[1]
    chosen = jnp.where(node == 0, pattern[0], pattern[1]).astype(jnp.float32)
    onehot = (
        jnp.arange(block_count, dtype=jnp.int32)[None, :] == (row_ids // BLK)[:, None]
    ).astype(jnp.float32)
    row_mask = jnp.sum(onehot * chosen[None, :], axis=1)[:, None]
    masked_coupling = coupling * row_mask
    lower_rows = lax.all_gather(root_lower, "cube", axis=1, tiled=True)
    root_cov = lax.psum_scatter(
        product(lower_rows.T, root_lower), "grid", scatter_dimension=0, tiled=True
    )
    cov_rows = lax.all_gather(root_cov, "cube", axis=1, tiled=True)
    other_coupling, other_lower = from_partner((masked_coupling, node_lower), "cube", 0)
    coupling_full = join_halves(masked_coupling, other_coupling, half)
    lower_full = join_halves(node_lower, other_lower, half)
    factor = product(coupling_full, lax.all_gather(node_lower, "grid", axis=0, tiled=True))
    cross = lax.psum_scatter(-product(cov_rows.T, factor), "grid", scatter_dimension=0, tiled=True)
    cross = cross * row_mask
    other_cross = from_partner(cross, "cube", 0)
    left_rows = join_halves(cross, other_cross, half)
    first = product(lower_full.T, node_lower)
    node_cov = lax.psum_scatter(
        first - product(left_rows.T, factor), "grid", scatter_dimension=0, tiled=True
    )
    return (root_cov, cross, node_cov)


def solution(mesh):
    placed = (P("grid", "cube"), P("grid", "cube"), P("grid", "cube"), P())
    return jax.shard_map(
        on_device,
        mesh=mesh,
        in_specs=placed,
        out_specs=(P("grid", "cube"), P("grid", "cube"), P("grid", "cube")),
        check_vma=False,
    )
```

profile of v0, /device:TPU:8, one launch (start us, length us, event | category | flops | bytes accessed | tf_op | source)
XLA Modules:
  0.0 671.0 jit_solution(15860373816275779728)
XLA Ops:
  7.2 1.8 select_add_fusion
  9.0 0.0 reduce-scatter.4.cloned.1.call-start
  9.1 29.8 %all-gather.4.cloned.1.call-done = f32[64,4096]{1,0:T(8,128)} async-done(((f32[64,1024]{1,0:T(8,128)}), f32[64,4096]{1,0:T(8,128)}) %all-gather.4.cloned.1.call-update) | async-done | bytes 1048592 | tf_op jit(solution)/shard_map/all_gather | solution.py:48
  38.9 16.9 %fusion.25 = f32[4096,1024]{1,0:T(8,128)} fusion(f32[64,4096]{1,0:T(8,128)} %all-gather.4.cloned.1.call-done, f32[64,1024]{1,0:T(8,128)} %select_add_fusion), kind=kOutput, calls=%fused_computation.45 | convolution fusion | flops 3221225472 | bytes 18087936 | tf_op jit(solution)/shard_map/dot_general | solution.py:15
  55.8 0.0 all-gather.8.cloned.1.call-start
  55.9 0.6 copy-done.3
  56.6 0.7 select_add_fusion.1
  57.3 189.2 %reduce-scatter.4.cloned.1.call-done = f32[64,1024]{1,0:T(8,128)} async-done(((f32[4096,1024]{1,0:T(8,128)}), f32[64,1024]{1,0:T(8,128)}) %reduce-scatter.4.cloned.1.call-update) | async-done | bytes 262160 | tf_op jit(solution)/shard_map/reduce_scatter | solution.py:49
  246.7 0.1 select_reduce_fusion
  246.8 0.1 broadcast_multiply_fusion.1
  246.9 0.6 collective-permute-start
  247.4 4.5 collective-permute-done
  251.9 73.5 %all-gather.8.cloned.1.call-done = f32[1024,512]{1,0:T(8,128)} async-done(((f32[16,512]{1,0:T(8,128)}), f32[1024,512]{1,0:T(8,128)}) %all-gather.8.cloned.1.call-update) | async-done | bytes 2097168 | tf_op jit(solution)/shard_map/all_gather | solution.py:56
  325.5 3.0 fusion
  328.4 22.7 %all-gather.6.cloned.1.call-done = f32[64,4096]{1,0:T(8,128)} async-done(((f32[64,1024]{1,0:T(8,128)}), f32[64,4096]{1,0:T(8,128)}) %all-gather.6.cloned.1.call-update) | async-done | bytes 1048592 | tf_op jit(solution)/shard_map/all_gather | solution.py:52
  351.1 10.0 %convolution_negate_fusion = f32[4096,512]{1,0:T(8,128)} fusion(f32[64,4096]{1,0:T(8,128)} %all-gather.6.cloned.1.call-done, f32[64,512]{1,0:T(8,128)S(1)} %fusion), kind=kOutput, calls=%fused_computation | convolution fusion | flops 1612709888 | bytes 9568256 | tf_op jit(solution)/shard_map/dot_general | solution.py:15
  361.2 152.8 %reduce-scatter.6.cloned.1.call-done = f32[64,512]{1,0:T(8,128)} async-done(((f32[4096,512]{1,0:T(8,128)}), f32[64,512]{1,0:T(8,128)}) %reduce-scatter.6.cloned.1.call-update) | async-done | bytes 131088 | tf_op jit(solution)/shard_map/reduce_scatter | solution.py:57
  514.0 1.0 broadcast_multiply_fusion
  514.9 0.6 collective-permute-start.2
  515.6 1.5 collective-permute-start.1
  517.1 2.9 collective-permute-done.2
  520.0 1.8 fusion.6
  521.9 3.2 convolution_subtract_fusion
  525.1 139.1 %reduce-scatter.8.cloned.1.call-done = f32[16,512]{1,0:T(8,128)} async-done(((f32[1024,512]{1,0:T(8,128)}), f32[16,512]{1,0:T(8,128)}) %reduce-scatter.8.cloned.1.call-update) | async-done | bytes 32784 | tf_op jit(solution)/shard_map/reduce_scatter | solution.py:62
  (26 shorter events, 0.3 us)
Async XLA Ops:
  7.2 31.7 %all-gather.4.cloned.1.call-start = ((), (), s32[]{:S(2)}) async-start(), calls=%async_computation.3 | async-start | bytes 1310720 | tf_op jit(solution)/shard_map/all_gather | solution.py:48
  9.0 237.5 %reduce-scatter.4.cloned.1.call-start = ((), (), s32[]{:S(2)}) async-start(), calls=%async_computation.4 | async-start | bytes 17039360 | tf_op jit(solution)/shard_map/reduce_scatter | solution.py:49
  55.8 0.8 copy-start.3
  55.8 190.9 %copy-start.4 = (s32[2,32]{1,0:T(2,128)S(1)}, s32[2,32]{1,0:T(2,128)}, u32[]{:S(2)}) copy-start(s32[2,32]{1,0:T(2,128)} %param.7) | copy-start | bytes 772
  55.8 191.0 %copy-start.2 = (f32[64,512]{1,0:T(8,128)S(1)}, f32[64,512]{1,0:T(8,128)}, u32[]{:S(2)}) copy-start(f32[64,512]{1,0:T(8,128)} %param.6) | copy-start | bytes 393220
  55.8 269.6 %all-gather.8.cloned.1.call-start = ((), (), s32[]{:S(2)}) async-start(), calls=%async_computation.6 | async-start | bytes 2129920 | tf_op jit(solution)/shard_map/all_gather | solution.py:56
  57.3 293.8 %all-gather.6.cloned.1.call-start = ((), (), s32[]{:S(2)}) async-start(), calls=%async_computation.5 | async-start | bytes 1310720 | tf_op jit(solution)/shard_map/all_gather | solution.py:52
  246.6 267.4 %reduce-scatter.6.cloned.1.call-start = ((), (), s32[]{:S(2)}) async-start(), calls=%async_computation.7 | async-start | bytes 8519680 | tf_op jit(solution)/shard_map/reduce_scatter | solution.py:57
  246.9 5.1 collective-permute-start
  361.1 154.5 %copy-start.1 = (f32[16,512]{1,0:T(8,128)S(1)}, f32[16,512]{1,0:T(8,128)}, u32[]{:S(2)}) copy-start(f32[16,512]{1,0:T(8,128)} %select_add_fusion.1) | copy-start | bytes 98308
  361.1 303.0 %reduce-scatter.8.cloned.1.call-start = ((), (), s32[]{:S(2)}) async-start(), calls=%async_computation.8 | async-start | bytes 2129920 | tf_op jit(solution)/shard_map/reduce_scatter | solution.py:62
  514.9 10.1 %copy-start = (f32[64,512]{1,0:T(8,128)}, f32[64,512]{1,0:T(8,128)S(1)}, u32[]{:S(2)}) copy-start(f32[64,512]{1,0:T(8,128)S(1)} %broadcast_multiply_fusion) | copy-start | bytes 393220
  514.9 5.1 collective-permute-start.2
  515.6 6.3 collective-permute-start.1
Sparse Core Ops, SparseCore 0:
  10.4 28.4 all-gather.3
  56.0 190.5 reduce-scatter.3
  249.9 75.4 all-gather.7
  327.7 23.3 all-gather.5
  361.3 152.6 reduce-scatter.5
  525.2 138.8 reduce-scatter.7
where the time goes:
time: 671 us
  waiting for transfers between devices  615 us (92%)
  matrix products  34.9 us (5%)
  between operations  14.2 us (2%)
    reduce_scatter x1, waiting for transfers between devices, on_device(): lax.psum_scatter(product(lower_rows.T, root_lower), 'grid', scatter_dimen...  189 us
    reduce_scatter x1, waiting for transfers between devices, on_device(): lax.psum_scatter(-product(cov_rows.T, factor), 'grid', scatter_dimension=...  153 us
    reduce_scatter x1, waiting for transfers between devices, on_device(): lax.psum_scatter(first - product(left_rows.T, factor), 'grid', scatter_di...  139 us
    all_gather x1, waiting for transfers between devices, on_device(): lax.all_gather(node_lower, 'grid', axis=0, tiled=True)  73.5 us
    dot_general x5, matrix products, product(): jnp.dot(left, right, precision=HIGHEST, preferred_element_type=jnp.float32)  34.9 us
    all_gather x1, waiting for transfers between devices, on_device(): lower_rows = lax.all_gather(root_lower, 'cube', axis=1, tiled=True)  29.8 us
    all_gather x1, waiting for transfers between devices, on_device(): cov_rows = lax.all_gather(root_cov, 'cube', axis=1, tiled=True)  22.7 us
  transfers between devices with their start and end apart: 9, of which 8 were waited for; matrix products, arithmetic and copies ran while one was open for 1% of the time, Pallas kernels for 0%

commit v1 on v0

--- a/solution.py
+++ b/solution.py
@@ -5,6 +5,28 @@
 
 BLK = 128
 HIGHEST = lax.Precision.HIGHEST
+
+
+def in_order(blocks, dim):
+    lengths = list(blocks.shape[1:])
+    lengths[dim] *= blocks.shape[0]
+    return jnp.moveaxis(blocks, 0, dim).reshape(lengths)
+
+
+def collect(x, axis, dim):
+    size = lax.axis_size(axis)
+    pairs = [(i, (i + 1) % size) for i in range(size)]
+    back = [(b, a) for a, b in pairs]
+    lower, upper = ([], [])
+    for step in range(size - 1):
+        if step % 2 == 0:
+            lower.append(lax.ppermute(lower[-1] if lower else x, axis, pairs))
+        else:
+            upper.append(lax.ppermute(upper[-1] if upper else x, axis, back))
+    tiles = jnp.stack([*lower[::-1], x, *upper])
+    shift = lax.axis_index(axis) - len(lower)
+    tiles = tiles[(jnp.arange(size) - shift) % size]
+    return in_order(tiles, dim)
 
 
 def from_partner(value, axis, apart):
@@ -49,7 +71,7 @@
     root_cov = lax.psum_scatter(
         product(lower_rows.T, root_lower), "grid", scatter_dimension=0, tiled=True
     )
-    cov_rows = lax.all_gather(root_cov, "cube", axis=1, tiled=True)
+    cov_rows = collect(root_cov, "cube", 1)
     other_coupling, other_lower = from_partner((masked_coupling, node_lower), "cube", 0)
     coupling_full = join_halves(masked_coupling, other_coupling, half)
     lower_full = join_halves(node_lower, other_lower, half)

time: 671 us -> 644 us (0.960)
  waiting for transfers between devices: 615 us -> 584 us
    all_gather x1 -> x0, waiting for transfers between devices: 22.7 us -> none  [on_device(): cov_rows = lax.all_gather(root_cov, 'cube', axis=1, tiled=True)]
  transfers between devices with their start and end apart: 9 -> 11, of which waited for: 8 -> 7; matrix products, arithmetic and copies ran while one was open for 1% -> 1% of each run, Pallas kernels for 0% -> 0%
where the time goes in v1:
time: 644 us
  waiting for transfers between devices  584 us (91%)
  matrix products  33.9 us (5%)
  between operations  14 us (2%)
  starting transfers between devices  7.42 us (1%)
    reduce_scatter x1, waiting for transfers between devices, on_device(): lax.psum_scatter(product(lower_rows.T, root_lower), 'grid', scatter_dimen...  189 us
    reduce_scatter x1, waiting for transfers between devices, on_device(): lax.psum_scatter(-product(cov_rows.T, factor), 'grid', scatter_dimension=...  149 us
    reduce_scatter x1, waiting for transfers between devices, on_device(): lax.psum_scatter(first - product(left_rows.T, factor), 'grid', scatter_di...  139 us
    all_gather x1, waiting for transfers between devices, on_device(): lax.all_gather(node_lower, 'grid', axis=0, tiled=True)  68.1 us
    dot_general x5, matrix products, product(): jnp.dot(left, right, precision=HIGHEST, preferred_element_type=jnp.float32)  33.9 us
    all_gather x1, waiting for transfers between devices, on_device(): lower_rows = lax.all_gather(root_lower, 'cube', axis=1, tiled=True)  29.8 us
  transfers between devices with their start and end apart: 11, of which 7 were waited for; matrix products, arithmetic and copies ran while one was open for 1% of the time, Pallas kernels for 0%

profile of v1, /device:TPU:8, one launch (start us, length us, event | category | flops | bytes accessed | tf_op | source)
XLA Modules:
  0.0 644.2 jit_solution(3449174010722368417)
XLA Ops:
  7.2 1.8 select_add_fusion
  9.1 29.8 %all-gather.3.cloned.1.call-done = f32[64,4096]{1,0:T(8,128)} async-done(((f32[64,1024]{1,0:T(8,128)}), f32[64,4096]{1,0:T(8,128)}) %all-gather.3.cloned.1.call-update) | async-done | bytes 1048592 | tf_op jit(solution)/shard_map/all_gather | solution.py:70
  38.9 16.9 %fusion.27 = f32[4096,1024]{1,0:T(8,128)} fusion(f32[64,4096]{1,0:T(8,128)} %all-gather.3.cloned.1.call-done, f32[64,1024]{1,0:T(8,128)} %select_add_fusion), kind=kOutput, calls=%fused_computation.54 | convolution fusion | flops 3221225472 | bytes 18087936 | tf_op jit(solution)/shard_map/dot_general | solution.py:37
  55.9 0.6 copy-done.4
  56.6 0.7 select_add_fusion.1
  57.5 189.1 %reduce-scatter.4.cloned.1.call-done = f32[64,1024]{1,0:T(8,128)} async-done(((f32[4096,1024]{1,0:T(8,128)}), f32[64,1024]{1,0:T(8,128)}) %reduce-scatter.4.cloned.1.call-update) | async-done | bytes 262160 | tf_op jit(solution)/shard_map/reduce_scatter | solution.py:71
  246.6 1.4 collective-permute-start
  248.1 0.7 collective-permute-start.3
  248.8 1.5 collective-permute-start.2
  250.3 5.5 collective-permute-done
  255.8 1.5 collective-permute-start.1
  257.3 68.1 %all-gather.5.cloned.1.call-done = f32[1024,512]{1,0:T(8,128)} async-done(((f32[16,512]{1,0:T(8,128)}), f32[1024,512]{1,0:T(8,128)}) %all-gather.5.cloned.1.call-update) | async-done | bytes 2097168 | tf_op jit(solution)/shard_map/all_gather | solution.py:78
  325.4 3.0 fusion
  328.5 0.1 pad_maximum_fusion
  328.6 0.6 gather_fusion
  329.3 9.0 %convolution_negate_fusion = f32[4096,512]{1,0:T(8,128)} fusion(f32[64,4096]{1,0:T(8,128)S(1)} %bitcast.18, f32[64,512]{1,0:T(8,128)S(1)} %fusion), kind=kOutput, calls=%fused_computation.1 | convolution fusion | flops 1612709888 | bytes 9568256 | tf_op jit(solution)/shard_map/dot_general | solution.py:37
  338.4 149.2 %reduce-scatter.6.cloned.1.call-done = f32[64,512]{1,0:T(8,128)} async-done(((f32[4096,512]{1,0:T(8,128)}), f32[64,512]{1,0:T(8,128)}) %reduce-scatter.6.cloned.1.call-update) | async-done | bytes 131088 | tf_op jit(solution)/shard_map/reduce_scatter | solution.py:79
  487.6 1.0 broadcast_multiply_fusion
  488.6 0.6 collective-permute-start.5
  489.2 1.5 collective-permute-start.4
  490.7 2.9 collective-permute-done.5
  493.7 1.8 fusion.6
  495.5 3.2 convolution_subtract_fusion
  498.7 139.0 %reduce-scatter.8.cloned.1.call-done = f32[16,512]{1,0:T(8,128)} async-done(((f32[1024,512]{1,0:T(8,128)}), f32[16,512]{1,0:T(8,128)}) %reduce-scatter.8.cloned.1.call-update) | async-done | bytes 32784 | tf_op jit(solution)/shard_map/reduce_scatter | solution.py:84
  (36 shorter events, 0.7 us)
Async XLA Ops:
  7.2 31.7 %all-gather.3.cloned.1.call-start = ((), (), s32[]{:S(2)}) async-start(), calls=%async_computation.3 | async-start | bytes 1310720 | tf_op jit(solution)/shard_map/all_gather | solution.py:70
  9.0 237.5 %reduce-scatter.4.cloned.1.call-start = ((), (), s32[]{:S(2)}) async-start(), calls=%async_computation.4 | async-start | bytes 17039360 | tf_op jit(solution)/shard_map/reduce_scatter | solution.py:71
  55.8 0.8 copy-start.4
  55.8 1.6 copy-start.5
  55.8 192.2 %copy-start.3 = (f32[64,512]{1,0:T(8,128)S(1)}, f32[64,512]{1,0:T(8,128)}, u32[]{:S(2)}) copy-start(f32[64,512]{1,0:T(8,128)} %param.6) | copy-start | bytes 393220
  55.8 269.6 %all-gather.5.cloned.1.call-start = ((), (), s32[]{:S(2)}) async-start(), calls=%async_computation.5 | async-start | bytes 2129920 | tf_op jit(solution)/shard_map/all_gather | solution.py:78
  57.3 430.3 %reduce-scatter.6.cloned.1.call-start = ((), (), s32[]{:S(2)}) async-start(), calls=%async_computation.6 | async-start | bytes 8519680 | tf_op jit(solution)/shard_map/reduce_scatter | solution.py:79
  246.6 81.9 %copy-start.2 = (f32[64,1024]{1,0:T(8,128)S(1)}, f32[64,1024]{1,0:T(8,128)}, u32[]{:S(2)}) copy-start(f32[64,1024]{1,0:T(8,128)} %reduce-scatter.4.cloned.1.call-done) | copy-start | bytes 786436
  246.6 9.3 %collective-permute-start = (f32[64,1024]{1,0:T(8,128)}, f32[64,1024]{1,0:T(8,128)S(1)}, u32[]{:S(2)}, u32[]{:S(2)}) collective-permute-start(f32[64,1024]{1,0:T(8,128)} %reduce-scatter.4.cloned.1.call-done), channel_id=1, source_target_pairs={{0,64},{64,128},{128,192},{192,0},{1,65},{65,129},{129,193},{193,1... | collective-permute-start | bytes 786440 | tf_op jit(solution)/shard_map/ppermute | solution.py:23
  248.1 9.3 %collective-permute-start.3 = (f32[64,512]{1,0:T(8,128)S(1)}, f32[64,512]{1,0:T(8,128)S(1)}, u32[]{:S(2)}, u32[]{:S(2)}) collective-permute-start(f32[64,512]{1,0:T(8,128)S(1)} %broadcast_multiply_fusion.1), channel_id=1, source_target_pairs={{0,64},{64,0},{128,192},{192,128},{1,65},{65,1},{129,193},{193,129... | collective-permute-start | bytes 393224 | tf_op jit(solution)/shard_map/ppermute | solution.py:33
  248.8 79.6 %collective-permute-start.2 = (f32[64,1024]{1,0:T(8,128)}, f32[64,1024]{1,0:T(8,128)S(1)}, u32[]{:S(2)}, u32[]{:S(2)}) collective-permute-start(f32[64,1024]{1,0:T(8,128)} %reduce-scatter.4.cloned.1.call-done), channel_id=1, source_target_pairs={{64,0},{128,64},{192,128},{0,192},{65,1},{129,65},{193,129},{1,193... | collective-permute-start | bytes 786440 | tf_op jit(solution)/shard_map/ppermute | solution.py:25
  255.8 72.6 %collective-permute-start.1 = (f32[64,1024]{1,0:T(8,128)S(1)}, f32[64,1024]{1,0:T(8,128)S(1)}, u32[]{:S(2)}, u32[]{:S(2)}) collective-permute-start(f32[64,1024]{1,0:T(8,128)S(1)} %collective-permute-done), channel_id=1, source_target_pairs={{0,64},{64,128},{128,192},{192,0},{1,65},{65,129},{129,193},{193,1... | collective-permute-start | bytes 786440 | tf_op jit(solution)/shard_map/ppermute | solution.py:23
  338.3 150.9 %copy-start.1 = (f32[16,512]{1,0:T(8,128)S(1)}, f32[16,512]{1,0:T(8,128)}, u32[]{:S(2)}) copy-start(f32[16,512]{1,0:T(8,128)} %select_add_fusion.1) | copy-start | bytes 98308
  338.3 299.4 %reduce-scatter.8.cloned.1.call-start = ((), (), s32[]{:S(2)}) async-start(), calls=%async_computation.7 | async-start | bytes 2129920 | tf_op jit(solution)/shard_map/reduce_scatter | solution.py:84
  488.6 10.1 %copy-start = (f32[64,512]{1,0:T(8,128)}, f32[64,512]{1,0:T(8,128)S(1)}, u32[]{:S(2)}) copy-start(f32[64,512]{1,0:T(8,128)S(1)} %broadcast_multiply_fusion) | copy-start | bytes 393220
  488.6 5.1 collective-permute-start.5
  489.2 6.3 collective-permute-start.4
Sparse Core Ops, SparseCore 0:
  10.4 28.4 all-gather.2
  56.0 190.5 reduce-scatter.3
  249.9 75.4 all-gather.4
  338.5 149.0 reduce-scatter.5
  498.8 138.8 reduce-scatter.7
